TPU v7x, 32 devices: a whole 2x2x4 slice. The times are simulated.
32 devices in a mesh: grp: 2 (over x), row: 16 (over z, y, core).
Axes of the slice: x: 2, y: 2, z: 4, core: 2. Of those that a mesh axis runs over, the one named last changes fastest.
Arguments:
- field: bfloat16 [256, 1024, 256], P(('grp', 'row')), parts along dimension 0, may hold values from -8 to 8, as said below
- w_qkv: bfloat16 [256, 768], replicated, may hold values from -0.375 to 0.375
- w_attn: bfloat16 [256, 256], replicated, may hold values from -0.375 to 0.375
- w_inner: bfloat16 [256, 512], replicated, may hold values from -0.375 to 0.375
- w_outer: bfloat16 [512, 256], replicated, may hold values from -0.25 to 0.25
- w_skip: bfloat16 [256, 256], replicated, may hold values from -0.375 to 0.375
- w_modes: bfloat16 [512, 2, 256, 256], P('row'), may hold values from -0.25 to 0.25
Outputs:
- result: bfloat16 [256, 1024, 256], P(('grp', 'row')), parts along dimension 0
There are 2 independent parts, one for each index of `grp`. A program takes and returns all parts, laid end to end along the dimension named above; an argument that names none is the same for every part. Nothing has to cross between parts.
Inputs may be any that keep to these rules, and one draw needn't show every extreme that they name: `field`: features of the slab's cells.
All inputs are finite; a program needn't handle non-finite values.
Results may differ from a plain program's by a relative error of at most 0.004.
The roundings to bfloat16 on the way count: a program that leaves them out, or rounds other values in their place, can miss the bound.
Values may be sent and summed in bfloat16 or wider, within the bound.
No kernel may reach another device: no remote copies, remote signals or barrier semaphores. Data moves between devices by JAX's collectives and lax.ppermute only.
A program may use at most 128 MiB of HBM per device.

v0:
```python
import functools

import jax
import jax.numpy as jnp
import numpy as np
from jax import lax
from jax.experimental import pallas as pl
from jax.experimental.pallas import tpu as pltpu
from jax.sharding import PartitionSpec as P

HEADS = 4
HD = 64
MH = 32
MW = 16
EPSILON = 1e-05
SUB = 512
KV_SUB = 256
LAST_SUB = 1024
ROWS = 2
F32 = jnp.float32
BF16 = jnp.bfloat16


def mm(a, b):
    return jnp.dot(a, b, preferred_element_type=F32)


def mm_nt(a, b):
    return lax.dot_general(a, b, (((1,), (1,)), ((), ())), preferred_element_type=F32)


def gelu(x):
    half = 0.5 * x
    return half + half * lax.erf(x * 0.7071067811865476)


def skewed(stages, count):
    held = [None] * count
    for at in range(count + len(stages) - 1):
        for k in reversed(range(len(stages))):
            if 0 <= at - k < count:
                held[at - k] = stages[k](at - k, held[at - k])


def column_table(columns):
    turns = np.arange(columns)[:, None] * np.arange(MW)[None, :] % columns
    angle = turns * (2 * np.pi / columns)
    return np.concatenate([np.cos(angle), -np.sin(angle)], axis=1)


def split(ref, at, value):
    for block in range(value.shape[1] // 128):
        ref[block, at, :] = value[:, block * 128 : (block + 1) * 128]


def join(ref, at, blocks):
    return jnp.concatenate([ref[block, at, :] for block in blocks], axis=1)


def halves(value):
    high = value.astype(BF16)
    return high, (value - np.asarray(high, np.float64)).astype(BF16)


def placing(size, per_owner, odd):
    if per_owner < MW:
        return list(range(MH))
    group = per_owner // MW
    owners = [*range(odd, size, 2), *range(1 - odd, size, 2)]
    return [owner * group + k for owner in owners for k in range(group)]


def rows_of(kw, per_owner, odd):
    if per_owner >= MW:
        return pl.ds(kw, MH, stride=MW)
    part = kw // per_owner
    first = ((part & 1) ^ odd) * (MH * MW // 2) + part // 2 * per_owner + kw % per_owner
    return pl.ds(first, MH, stride=MW // 2)


def row_tables(size, strip_rows, per_owner):
    height = size * strip_rows
    ahead, back = [], []
    for me in range(size):
        order = np.array(placing(size, per_owner, me & 1))
        freqs = np.where(order < MH // 2, order, order - MH + height)
        angle = freqs[:, None] * (me * strip_rows + np.arange(strip_rows))[None, :] % height * (2 * np.pi / height)
        cos, sin = np.cos(angle), np.sin(angle)
        real = np.stack([cos, sin], axis=2).reshape(MH, -1)
        imag = np.stack([-sin, cos], axis=2).reshape(MH, -1)
        high, low = halves(np.concatenate([real, imag]))
        ahead.append(np.concatenate([high, high, low], axis=1))
        real = np.concatenate([cos, -sin]).T
        imag = np.concatenate([sin, cos]).T
        back.append(np.concatenate(halves(np.stack([real, imag], axis=1).reshape(2 * strip_rows, -1)), axis=1))
    return np.stack(ahead), np.stack(back)


def kv_kernel(me_ref, far_ref, w_far, wa_ref, wi_ref, wo_ref, keep_ref, send_ref, x_ref, w_ref, wa_near, wi_near, wo_near,
              w_t, normed, acc, arrived, landed):
    step = pl.program_id(0)
    channels = HEADS * HD
    fetches = [
        pltpu.make_async_copy(far, to, arrived.at[i])
        for i, (far, to) in enumerate(((wa_ref, wa_near), (wi_ref, wi_near), (wo_ref, wo_near)))
    ]

    def row_copy(row):
        return pltpu.make_async_copy(far_ref.at[row], x_ref.at[row], landed.at[row])

    @pl.when(step == 0)
    def _():
        weights = pltpu.make_async_copy(w_far, w_ref, arrived.at[3])
        weights.start()
        for row in range(x_ref.shape[0]):
            row_copy(row).start()
        for fetch in fetches:
            fetch.start()
        normed[...] = jnp.zeros_like(normed)
        acc[...] = jnp.zeros_like(acc)
        weights.wait()
        w_t[...] = w_ref[:, channels:].T

    row_copy(step).wait()
    acc[...] += mm_nt(normed[:channels, :], normed[channels:, :])

    def project(block, _):
        return mm_nt(w_t[...], x_ref[step, block * KV_SUB : (block + 1) * KV_SUB, :])

    def normalize(block, both):
        shaped = both.reshape(2 * HEADS, HD, KV_SUB)
        center = shaped - jnp.sum(shaped, axis=1, keepdims=True) * (1.0 / HD)
        spread = jnp.sum(center * center, axis=1, keepdims=True) * (1.0 / HD) + EPSILON
        scaled = center * lax.rsqrt(spread)
        normed[:, block * KV_SUB : (block + 1) * KV_SUB] = scaled.reshape(2 * channels, KV_SUB).astype(BF16)

    skewed([project, normalize], x_ref.shape[1] // KV_SUB)

    @pl.when(step == pl.num_programs(0) - 1)
    def _():
        total = acc[...] + mm_nt(normed[:channels, :], normed[channels:, :])
        left = lax.broadcasted_iota(jnp.int32, (HD, 2 * HD), 1) < HD
        pairs = []
        for row in range(0, channels, 2 * HD):
            cols = slice(row, row + 2 * HD)
            pairs.append(jnp.where(left, total[row : row + HD, cols], total[row + HD : row + 2 * HD, cols]))
        odd = me_ref[0] == 1
        keep_ref[...] = jnp.where(odd, pairs[1], pairs[0])
        send_ref[...] = jnp.where(odd, pairs[0], pairs[1])
        for fetch in fetches:
            fetch.wait()


def query_kernel(x_ref, w_ref, out_ref):
    step = pl.program_id(0)
    out_ref[step] = mm(x_ref[step], w_ref[:, : x_ref.shape[2]]).astype(BF16)


def field_kernel(cells, me_ref, x_ref, kva_ref, kvb_ref, ask_ref, wa_ref, wi_ref, wo_ref, tab_ref, ang_ref, far_ref,
                 second_ref, keep_ref, send_ref, near_ref, scaled, spectra, terms, arrived):
    step = pl.program_id(0)
    rows = x_ref.shape[0]
    fetch = pltpu.make_async_copy(far_ref, near_ref, arrived)

    @pl.when(step == 0)
    def _():
        fetch.start()
        odd = me_ref[0] == 1
        mine, theirs = kva_ref[...] / cells, kvb_ref[...] / cells
        packed = (jnp.where(odd, theirs, mine), jnp.where(odd, mine, theirs))
        left = lax.broadcasted_iota(jnp.int32, (HD, 2 * HD), 1) < HD
        blank = jnp.zeros((HD, 2 * HD), F32)
        blocks = []
        for pair in range(HEADS // 2):
            part = packed[pair]
            for mine in (jnp.where(left, part, 0.0), jnp.where(left, 0.0, part)):
                line = [blank] * (HEADS // 2)
                line[pair] = mine
                blocks.append(jnp.concatenate(line, axis=1))
        scaled[...] = jnp.concatenate(blocks, axis=0).astype(BF16)

    columns = x_ref.shape[1]
    per_row = columns // SUB

    def place(block):
        return step * ROWS + block // per_row, slice(block % per_row * SUB, (block % per_row + 1) * SUB)

    def attend(block, _):
        row, here = place(block)
        return mm(ask_ref[row, here, :], scaled[...]).astype(BF16)

    def add(block, attended):
        row, here = place(block)
        return (x_ref[row, here, :].astype(F32) + mm(attended, wa_ref[...])).astype(BF16)

    def widen(block, first):
        return first, gelu(mm(first, wi_ref[...])).astype(BF16)

    def narrow(block, pair):
        row, here = place(block)
        first, hidden = pair
        second_ref[row, here, :] = (first.astype(F32) + mm(hidden, wo_ref[...])).astype(BF16)
        if block % per_row == per_row - 1:
            transform(row)

    def transform(row):
        at = pl.ds(pl.multiple_of(row * 2 * MW, 2 * MW), 2 * MW)
        split(spectra, at, mm(tab_ref[...], second_ref[row]))

    skewed([attend, add, widen, narrow], ROWS * per_row)

    @pl.when(step == pl.num_programs(0) - 1)
    def _():
        per_owner = keep_ref.shape[1]
        for kw in range(MW):
            spectrum = join(spectra, pl.ds(kw, 2 * rows, stride=MW), range(spectra.shape[0]))
            high = spectrum.astype(BF16)
            low = (spectrum - high.astype(F32)).astype(BF16)
            found = mm(ang_ref[me_ref[1]], jnp.concatenate([high, low, high], axis=0))
            at = rows_of(kw, per_owner, me_ref[0])
            split(terms, at, jnp.concatenate([found[:MH], found[MH:]], axis=1))
        fetch.wait()
        middle = MH * MW // 2
        for block in range(terms.shape[0]):
            here = slice(block * 128, (block + 1) * 128)
            keep_ref[:, :, here] = terms[block, :middle].reshape(keep_ref.shape[:2] + (128,))
            send_ref[:, :, here] = terms[block, middle:].astype(BF16).reshape(keep_ref.shape[:2] + (128,))


def mode_kernel(terms_ref, w_ref, out_ref):
    step = pl.program_id(0)
    group = 8
    channels = HEADS * HD
    rows = pl.ds(pl.multiple_of(step * group, group), group)
    coeff = jnp.sum(terms_ref[:, rows, :].astype(F32), axis=0).astype(BF16).astype(F32)
    re, im = coeff[:, :channels], coeff[:, channels:]
    lhs = jnp.concatenate(
        [jnp.concatenate([re, -im], axis=1), jnp.concatenate([im, re], axis=1)], axis=0
    ).astype(BF16)
    index = lax.broadcasted_iota(jnp.int32, (2 * group, channels), 0) % group
    mixed = jnp.zeros((2 * group, channels), F32)
    for m in range(group):
        mixed = jnp.where(index == m, mm(lhs, w_ref[step * group + m]), mixed)
    for copy in range(out_ref.shape[0]):
        out_ref[copy, rows, :channels] = mixed[:group].astype(BF16)
        out_ref[copy, rows, channels:] = mixed[group:].astype(BF16)


def last_kernel(cells, me_ref, second_ref, lo_ref, hi_ref, ws_ref, tab_ref, ang_ref, out_ref, mixed, back, held, sent):
    step = pl.program_id(0)
    channels = HEADS * HD
    rows = second_ref.shape[0]

    @pl.when(step == 0)
    def _():
        per_owner = lo_ref.shape[1]
        middle = MH * MW // 2
        split(mixed, slice(0, middle), lo_ref[...].astype(F32).reshape(middle, 2 * channels))
        split(mixed, slice(middle, None), hi_ref[...].astype(F32).reshape(middle, 2 * channels))
        for kw in range(MW):
            at = rows_of(kw, per_owner, me_ref[0])
            blocks = range(mixed.shape[0])
            re, im = join(mixed, at, blocks[: len(blocks) // 2]), join(mixed, at, blocks[len(blocks) // 2 :])
            both = jnp.concatenate([re, im], axis=0).astype(BF16)
            found = mm(ang_ref[me_ref[1]], jnp.concatenate([both, both], axis=0))
            split(back, pl.ds(kw, 2 * rows, stride=MW), found * ((2.0 if kw else 1.0) / cells))

    there = pl.ds(pl.multiple_of(step * 2 * MW, 2 * MW), 2 * MW)
    rhs = jnp.concatenate([ws_ref[...], join(back, there, range(back.shape[0])).astype(BF16)], axis=0)

    def both(block, _):
        here = slice(block * LAST_SUB, (block + 1) * LAST_SUB)
        return mm(jnp.concatenate([second_ref[step, here, :], tab_ref[here, :]], axis=1), rhs)

    blocks = second_ref.shape[1] // LAST_SUB

    def send(row, block):
        here = pl.ds(block * LAST_SUB, LAST_SUB)
        return pltpu.make_async_copy(held.at[row, here], out_ref.at[row, here], sent.at[row, block])

    def finish(block, value):
        held[step, block * LAST_SUB : (block + 1) * LAST_SUB, :] = gelu(value).astype(BF16)
        send(step, block).start()

    skewed([both, finish], blocks)

    @pl.when(step == pl.num_programs(0) - 1)
    def _():
        for row in range(rows):
            for block in range(blocks):
                send(row, block).wait()


def near(value):
    return pltpu.with_memory_space_constraint(value, pltpu.VMEM)


def away(value):
    return pltpu.with_memory_space_constraint(value, pltpu.HBM)


HERE = pl.BlockSpec(memory_space=pltpu.VMEM)


def local(field, w_qkv, w_attn, w_inner, w_outer, w_skip, w_modes):
    strip_rows, columns, channels = field.shape
    size = lax.axis_size("row")
    bits = size.bit_length() - 1
    assert size == 1 << bits and size > 1
    me = lax.axis_index("row")
    height = strip_rows * size
    cells = float(height * columns)
    per_owner = w_modes.shape[0]
    ids = jnp.stack([me & 1, me]).astype(jnp.int32)
    chips = [list(range(core, size, 2)) for core in (0, 1)]

    def swap(value, distance):
        return lax.ppermute(value, "row", [(i, i ^ distance) for i in range(size)])

    table = column_table(columns)
    wide = jnp.asarray(table.T, BF16)
    tall = jnp.asarray(table, BF16)
    ahead, behind = (jnp.asarray(t) for t in row_tables(size, strip_rows, per_owner))

    kv_shape = (HD, 2 * HD)
    hbm = pl.BlockSpec(memory_space=pltpu.HBM)
    keep, send, x_near, wq_near, wa_near, wi_near, wo_near = pl.pallas_call(
        kv_kernel,
        out_shape=[pltpu.VMEM(kv_shape, F32)] * 2 + [pltpu.VMEM(w.shape, BF16) for w in (field, w_qkv, w_attn, w_inner, w_outer)],
        grid_spec=pltpu.PrefetchScalarGridSpec(
            num_scalar_prefetch=1,
            grid=(strip_rows,),
            in_specs=[hbm] * 5,
            out_specs=[HERE] * 7,
            scratch_shapes=[
                pltpu.VMEM((2 * channels, channels), BF16),
                pltpu.VMEM((2 * channels, columns), BF16),
                pltpu.VMEM((channels, channels), F32),
                pltpu.SemaphoreType.DMA((4,)),
                pltpu.SemaphoreType.DMA((strip_rows,)),
            ],
        ),
        compiler_params=pltpu.CompilerParams(vmem_limit_bytes=12 << 20),
        name="kv",
    )(ids, away(field), away(w_qkv), away(w_attn), away(w_inner), away(w_outer))
    queries = pl.pallas_call(
        query_kernel,
        out_shape=pltpu.VMEM(field.shape, BF16),
        grid=(strip_rows,),
        in_specs=[HERE, HERE],
        out_specs=HERE,
        compiler_params=pltpu.CompilerParams(vmem_limit_bytes=4 << 20),
        cost_estimate=pl.CostEstimate(
            flops=2 * field.size * channels, bytes_accessed=4 * field.size, transcendentals=0
        ),
        name="qproj",
    )(near(x_near), near(wq_near))
    kv = keep + swap(send, 1)
    for b in range(1, bits, 2):
        steps = [1 << b] if b + 1 == bits else [1 << b, 2 << b, 3 << b]
        others = []
        for d in steps:
            others.append(swap(kv, d))
        kv = sum(others, kv)
    other = swap(kv, 1)

    half = (size // 2, per_owner, 2 * channels)
    mode_shape = (per_owner, 2 * channels, channels)
    second, keep, send, w_near = pl.pallas_call(
        functools.partial(field_kernel, cells),
        out_shape=[
            pltpu.VMEM(field.shape, BF16),
            pltpu.VMEM(half, F32),
            pltpu.VMEM(half, BF16),
            pltpu.VMEM(mode_shape, BF16),
        ],
        grid_spec=pltpu.PrefetchScalarGridSpec(
            num_scalar_prefetch=1,
            grid=(strip_rows // ROWS,),
            in_specs=[HERE] * 9 + [hbm],
            out_specs=[HERE, HERE, HERE, HERE],
            scratch_shapes=[
                pltpu.VMEM((channels, channels), BF16),
                pltpu.VMEM((channels // 128, strip_rows * 2 * MW, 128), F32),
                pltpu.VMEM((channels // 64, MH * MW, 128), F32),
                pltpu.SemaphoreType.DMA(()),
            ],
        ),
        compiler_params=pltpu.CompilerParams(vmem_limit_bytes=14 << 20),
        name="field",
    )(ids, *map(near, (x_near, kv, other, queries, wa_near, wi_near, wo_near, wide, ahead)), away(w_modes.reshape(mode_shape)))

    both = (keep + swap(send, 1).astype(F32)).astype(BF16)
    terms = lax.all_to_all(both, "row", 0, 0, axis_index_groups=chips, tiled=True)

    group = 8
    copies = pl.pallas_call(
        mode_kernel,
        out_shape=pltpu.VMEM(half, BF16),
        grid=(per_owner // group,),
        in_specs=[HERE, HERE],
        out_specs=HERE,
        compiler_params=pltpu.CompilerParams(vmem_limit_bytes=4 << 20),
        name="modes",
    )(near(terms), near(w_near))

    held = lax.all_to_all(copies, "row", 0, 0, axis_index_groups=chips, tiled=True)
    far = swap(held, 1)

    return pl.pallas_call(
        functools.partial(last_kernel, cells),
        out_shape=jax.ShapeDtypeStruct(field.shape, BF16),
        grid_spec=pltpu.PrefetchScalarGridSpec(
            num_scalar_prefetch=1,
            grid=(strip_rows,),
            in_specs=[HERE] * 6,
            out_specs=hbm,
            scratch_shapes=[
                pltpu.VMEM((channels // 64, MH * MW, 128), F32),
                pltpu.VMEM((channels // 128, strip_rows * 2 * MW, 128), F32),
                pltpu.VMEM(field.shape, BF16),
                pltpu.SemaphoreType.DMA((strip_rows, columns // LAST_SUB)),
            ],
        ),
        compiler_params=pltpu.CompilerParams(vmem_limit_bytes=12 << 20),
        name="last",
    )(ids, *map(near, (second, held, far, w_skip, tall, behind)))


def solution(mesh):
    placed = (P(("grp", "row"), None, None), P(), P(), P(), P(), P(), P("row", None, None, None))
    return jax.shard_map(local, mesh=mesh, in_specs=placed, out_specs=P(("grp", "row"), None, None), check_vma=False)
```

profile of v0, /device:TPU:0, one launch (start us, length us, event | category | flops | bytes accessed | tf_op | source)
XLA Modules:
  0.0 74.5 jit_solution(4720507837734700835)
XLA Ops:
  0.0 0.1 pad_add_fusion.me_ref
  0.1 9.4 %kv.1 = (f32[64,128]{1,0:T(8,128)S(1)}, f32[64,128]{1,0:T(8,128)S(1)}, bf16[8,1024,256]{2,1,0:T(8,128)(2,1)S(1)}, bf16[256,768]{1,0:T(8,128)(2,1)S(1)}, bf16[256...) custom-call(s32[2]{0:T(128)S(1)} %pad_add_fusion.me_ref, ...), custom_call_target="tpu_custom_call" | custom-call | tf_op jit(solution)/shard_map/kv/pallas_call | solution.py:327
  9.4 0.6 collective-permute-start
  10.0 0.9 %collective-permute-done = f32[64,128]{1,0:T(8,128)S(1)} collective-permute-done((f32[64,128]{1,0:T(8,128)S(1)}, f32[64,128]{1,0:T(8,128)S(1)}, u32[]{:S(2)}, u32[]{:S(2)}) %collective-permute-start) | collective-permute-done | bytes 32800 | tf_op jit(solution)/shard_map/ppermute | solution.py:318
  10.9 3.9 %collective-permute-start.3 = (f32[64,128]{1,0:T(8,128)S(1)}, f32[64,128]{1,0:T(8,128)S(1)}, u32[]{:S(2)}, u32[]{:S(2)}) collective-permute-start(f32[64,128]{1,0:T(8,128)S(1)} %add.18), channel_id=1, source_target_pairs={{0,6},{1,7},{2,4},{3,5},{4,2},{5,3},{6,0},{7,1},{8,14},{9,15},{10,... | collective-permute-start | bytes 98312 | tf_op jit(solution)/shard_map/ppermute | solution.py:318
  14.7 0.5 collective-permute-start.2
  15.2 0.2 collective-permute-start.1
  15.4 1.3 %collective-permute-done.3 = f32[64,128]{1,0:T(8,128)S(1)} collective-permute-done((f32[64,128]{1,0:T(8,128)S(1)}, f32[64,128]{1,0:T(8,128)S(1)}, u32[]{:S(2)}, u32[]{:S(2)}) %collective-permute-start.3) | collective-permute-done | bytes 32800 | tf_op jit(solution)/shard_map/ppermute | solution.py:318
  16.6 2.0 %collective-permute-done.2 = f32[64,128]{1,0:T(8,128)S(1)} collective-permute-done((f32[64,128]{1,0:T(8,128)S(1)}, f32[64,128]{1,0:T(8,128)S(1)}, u32[]{:S(2)}, u32[]{:S(2)}) %collective-permute-start.2) | collective-permute-done | bytes 32800 | tf_op jit(solution)/shard_map/ppermute | solution.py:318
  18.7 0.5 collective-permute-done.1
  19.1 2.6 %collective-permute-start.4 = (f32[64,128]{1,0:T(8,128)S(1)}, f32[64,128]{1,0:T(8,128)S(1)}, u32[]{:S(2)}, u32[]{:S(2)}) collective-permute-start(f32[64,128]{1,0:T(8,128)S(1)} %add_add_fusion), channel_id=1, source_target_pairs={{0,8},{1,9},{2,10},{3,11},{4,12},{5,13},{6,14},{7,15},{8,0},{9,1},... | collective-permute-start | bytes 98312 | tf_op jit(solution)/shard_map/ppermute | solution.py:318
  21.8 2.2 %collective-permute-done.4 = f32[64,128]{1,0:T(8,128)S(1)} collective-permute-done((f32[64,128]{1,0:T(8,128)S(1)}, f32[64,128]{1,0:T(8,128)S(1)}, u32[]{:S(2)}, u32[]{:S(2)}) %collective-permute-start.4) | collective-permute-done | bytes 32800 | tf_op jit(solution)/shard_map/ppermute | solution.py:318
  24.0 0.0 collective-permute-start.5
  24.0 0.0 copy-start
  24.0 0.0 copy-start.4
  24.0 2.4 %qproj.1.ask_ref = bf16[8,1024,256]{2,1,0:T(8,128)(2,1)S(1)} custom-call(bf16[8,1024,256]{2,1,0:T(8,128)(2,1)S(1)} %get-tuple-element.16.x_ref, bf16[256,768]{1,0:T(8,128)(2,1)S(1)} %get-tuple-element.19.w_ref), custom_call_target="tpu_custom_call" | custom-call | flops 1073741824 | bytes 8388608 | tf_op jit(solution)/shard_map/qproj/pallas_call | solution.py:346
  26.4 0.0 collective-permute-done.5.kvb_ref
  26.4 0.0 copy-done
  26.5 0.0 copy-done.4
  26.5 10.9 %field.1 = (bf16[8,1024,256]{2,1,0:T(8,128)(2,1)S(1)}, f32[8,32,512]{2,1,0:T(8,128)S(1)}, bf16[8,32,512]{2,1,0:T(8,128)(2,1)S(1)}, bf16[32,512,256]{2,1,0:T(8,128)(2,1)S(1)}) custom-call(s32[2]{0:T(128)S(1)} %pad_add_fusion.me_ref, bf16[8,1024,256]{2,1,0:T(8,128)(2,1)S(1)} %get-tuple-element.16.x_ref, f32[64,128]{1,0:T(8,128)S(1)} %add.22.kva_ref, ...), custom_call_target="tpu_custom_call" | custom-call | tf_op jit(solution)/shard_map/field/pallas_call | solution.py:369
  37.3 0.6 collective-permute-start.6
  37.9 1.2 %collective-permute-done.6 = bf16[8,32,512]{2,1,0:T(8,128)(2,1)S(1)} collective-permute-done((bf16[8,32,512]{2,1,0:T(8,128)(2,1)S(1)}, bf16[8,32,512]{2,1,0:T(8,128)(2,1)S(1)}, u32[]{:S(2)}, u32[]{:S(2)}) %collective-permute-start.6) | collective-permute-done | bytes 262176 | tf_op jit(solution)/shard_map/ppermute | solution.py:318
  39.1 0.1 add_convert_fusion
  39.1 14.3 %all_to_all.10.terms_ref = bf16[8,32,512]{2,1,0:T(8,128)(2,1)S(1)} all-to-all(bf16[8,32,512]{2,1,0:T(8,128)(2,1)S(1)} %add_convert_fusion), channel_id=1, replica_groups={{0,2,4,6,8,10,12,14},{1,3,5,7,9,11,13,15},{16,18,20,22,24,26,28,30},{17..., dimensions={0} | all-to-all | bytes 524288 | tf_op jit(solution)/shard_map/all_to_all | solution.py:394
  53.5 1.6 %modes.1 = bf16[8,32,512]{2,1,0:T(8,128)(2,1)S(1)} custom-call(bf16[8,32,512]{2,1,0:T(8,128)(2,1)S(1)} %all_to_all.10.terms_ref, bf16[32,512,256]{2,1,0:T(8,128)(2,1)S(1)} %get-tuple-element.26.w_ref), custom_call_target="tpu_custom_call" | custom-call | tf_op jit(solution)/shard_map/modes/pallas_call | solution.py:397
  55.0 12.4 %all_to_all.11.lo_ref = bf16[8,32,512]{2,1,0:T(8,128)(2,1)S(1)} all-to-all(bf16[8,32,512]{2,1,0:T(8,128)(2,1)S(1)} %modes.1), channel_id=1, replica_groups={{0,2,4,6,8,10,12,14},{1,3,5,7,9,11,13,15},{16,18,20,22,24,26,28,30},{17..., dimensions={0} | all-to-all | bytes 524288 | tf_op jit(solution)/shard_map/all_to_all | solution.py:407
  67.4 0.0 collective-permute-start.7
  67.5 1.5 %collective-permute-done.7.hi_ref = bf16[8,32,512]{2,1,0:T(8,128)(2,1)S(1)} collective-permute-done((bf16[8,32,512]{2,1,0:T(8,128)(2,1)S(1)}, bf16[8,32,512]{2,1,0:T(8,128)(2,1)S(1)}, u32[]{:S(2)}, u32[]{:S(2)}) %collective-permute-start.7) | collective-permute-done | bytes 262176 | tf_op jit(solution)/shard_map/ppermute | solution.py:318
  69.0 0.0 copy-done.1
  69.0 0.0 copy-done.2
  69.0 0.0 copy-done.3
  69.0 5.5 %last.1 = bf16[8,1024,256]{2,1,0:T(8,128)(2,1)} custom-call(s32[2]{0:T(128)S(1)} %pad_add_fusion.me_ref, bf16[8,1024,256]{2,1,0:T(8,128)(2,1)S(1)} %get-tuple-element.23.second_ref, bf16[8,32,512]{2,1,0:T(8,128)(2,1)S(1)} %all_to_all.11.lo_ref, bf16[8,32,512]{2,1,0:T(8,128)(2,1)S(1)} %collective-permute-done.7.hi_ref, bf16[256,256]{1,0:T(8,128)(2,1)S(1)} %copy-done.2, ...), custom_call_target="tpu_custom_call" | custom-call | tf_op jit(solution)/shard_map/last/pallas_call | solution.py:410
  (6 shorter events, 0.0 us)
Async XLA Ops:
  9.4 1.4 %collective-permute-start = (f32[64,128]{1,0:T(8,128)S(1)}, f32[64,128]{1,0:T(8,128)S(1)}, u32[]{:S(2)}, u32[]{:S(2)}) collective-permute-start(f32[64,128]{1,0:T(8,128)S(1)} %get-tuple-element.18), channel_id=1, source_target_pairs={{0,1},{1,0},{2,3},{3,2},{4,5},{5,4},{6,7},{7,6},{8,9},{9,8},{10,11... | collective-permute-start | bytes 98312 | tf_op jit(solution)/shard_map/ppermute | solution.py:318
  10.9 5.8 %collective-permute-start.3 = (f32[64,128]{1,0:T(8,128)S(1)}, f32[64,128]{1,0:T(8,128)S(1)}, u32[]{:S(2)}, u32[]{:S(2)}) collective-permute-start(f32[64,128]{1,0:T(8,128)S(1)} %add.18), channel_id=1, source_target_pairs={{0,6},{1,7},{2,4},{3,5},{4,2},{5,3},{6,0},{7,1},{8,14},{9,15},{10,... | collective-permute-start | bytes 98312 | tf_op jit(solution)/shard_map/ppermute | solution.py:318
  14.7 3.9 %collective-permute-start.2 = (f32[64,128]{1,0:T(8,128)S(1)}, f32[64,128]{1,0:T(8,128)S(1)}, u32[]{:S(2)}, u32[]{:S(2)}) collective-permute-start(f32[64,128]{1,0:T(8,128)S(1)} %add.18), channel_id=1, source_target_pairs={{0,4},{1,5},{2,6},{3,7},{4,0},{5,1},{6,2},{7,3},{8,12},{9,13},{10,... | collective-permute-start | bytes 98312 | tf_op jit(solution)/shard_map/ppermute | solution.py:318
  15.2 3.9 %collective-permute-start.1 = (f32[64,128]{1,0:T(8,128)S(1)}, f32[64,128]{1,0:T(8,128)S(1)}, u32[]{:S(2)}, u32[]{:S(2)}) collective-permute-start(f32[64,128]{1,0:T(8,128)S(1)} %add.18), channel_id=1, source_target_pairs={{0,2},{1,3},{2,0},{3,1},{4,6},{5,7},{6,4},{7,5},{8,10},{9,11},{10,... | collective-permute-start | bytes 98312 | tf_op jit(solution)/shard_map/ppermute | solution.py:318
  19.1 4.9 %collective-permute-start.4 = (f32[64,128]{1,0:T(8,128)S(1)}, f32[64,128]{1,0:T(8,128)S(1)}, u32[]{:S(2)}, u32[]{:S(2)}) collective-permute-start(f32[64,128]{1,0:T(8,128)S(1)} %add_add_fusion), channel_id=1, source_target_pairs={{0,8},{1,9},{2,10},{3,11},{4,12},{5,13},{6,14},{7,15},{8,0},{9,1},... | collective-permute-start | bytes 98312 | tf_op jit(solution)/shard_map/ppermute | solution.py:318
  24.0 2.4 %collective-permute-start.5 = (f32[64,128]{1,0:T(8,128)S(1)}, f32[64,128]{1,0:T(8,128)S(1)}, u32[]{:S(2)}, u32[]{:S(2)}) collective-permute-start(f32[64,128]{1,0:T(8,128)S(1)} %add.22.kva_ref), channel_id=1, source_target_pairs={{0,1},{1,0},{2,3},{3,2},{4,5},{5,4},{6,7},{7,6},{8,9},{9,8},{10,11... | collective-permute-start | bytes 98312 | tf_op jit(solution)/shard_map/ppermute | solution.py:318
  24.0 2.4 %copy-start = (bf16[16,64,48]{2,1,0:T(8,128)(2,1)S(1)}, bf16[16,64,48]{2,1,0:T(8,128)(2,1)}, u32[]{:S(2)}) copy-start(bf16[16,64,48]{2,1,0:T(8,128)(2,1)} %constant.16.clone.ang_ref) | copy-start | bytes 294916
  24.0 2.4 %copy-start.4 = (bf16[32,1024]{1,0:T(8,128)(2,1)S(1)}, bf16[32,1024]{1,0:T(8,128)(2,1)}, u32[]{:S(2)}) copy-start(bf16[32,1024]{1,0:T(8,128)(2,1)} %constant.14.clone.tab_ref) | copy-start | bytes 196612
  37.3 1.7 %collective-permute-start.6 = (bf16[8,32,512]{2,1,0:T(8,128)(2,1)S(1)}, bf16[8,32,512]{2,1,0:T(8,128)(2,1)S(1)}, u32[]{:S(2)}, u32[]{:S(2)}) collective-permute-start(bf16[8,32,512]{2,1,0:T(8,128)(2,1)S(1)} %get-tuple-element.25), channel_id=1, source_target_pairs={{0,1},{1,0},{2,3},{3,2},{4,5},{5,4},{6,7},{7,6},{8,9},{9,8},{10,11... | collective-permute-start | bytes 786440 | tf_op jit(solution)/shard_map/ppermute | solution.py:318
  53.5 15.5 %copy-start.1 = (bf16[1024,32]{1,0:T(8,128)(2,1)S(1)}, bf16[1024,32]{1,0:T(8,128)(2,1)}, u32[]{:S(2)}) copy-start(bf16[1024,32]{1,0:T(8,128)(2,1)} %constant.15.clone.tab_ref) | copy-start | bytes 196612
  53.5 15.5 %copy-start.2 = (bf16[256,256]{1,0:T(8,128)(2,1)S(1)}, bf16[256,256]{1,0:T(8,128)(2,1)}, u32[]{:S(2)}) copy-start(bf16[256,256]{1,0:T(8,128)(2,1)} %ws_ref.1) | copy-start | bytes 393220
  53.5 15.5 %copy-start.3 = (bf16[16,16,128]{2,1,0:T(8,128)(2,1)S(1)}, bf16[16,16,128]{2,1,0:T(8,128)(2,1)}, u32[]{:S(2)}) copy-start(bf16[16,16,128]{2,1,0:T(8,128)(2,1)} %constant.17.clone.ang_ref) | copy-start | bytes 196612
  67.4 1.5 %collective-permute-start.7 = (bf16[8,32,512]{2,1,0:T(8,128)(2,1)S(1)}, bf16[8,32,512]{2,1,0:T(8,128)(2,1)S(1)}, u32[]{:S(2)}, u32[]{:S(2)}) collective-permute-start(bf16[8,32,512]{2,1,0:T(8,128)(2,1)S(1)} %all_to_all.11.lo_ref), channel_id=1, source_target_pairs={{0,1},{1,0},{2,3},{3,2},{4,5},{5,4},{6,7},{7,6},{8,9},{9,8},{10,11... | collective-permute-start | bytes 786440 | tf_op jit(solution)/shard_map/ppermute | solution.py:318
where the time goes:
time: 74.7 us; the launch traced here: 74.5 us
  Pallas kernels  29.7 us (40%)
  blocking collectives  26.7 us (36%)
  waiting for transfers between devices  9.51 us (13%)
  starting transfers between devices  8.28 us (11%)
    all_to_all x1, blocking collectives, local(): lax.all_to_all(both, 'row', 0, 0, axis_index_groups=chips, tiled=True)  14.3 us
    all_to_all x1, blocking collectives, local(): lax.all_to_all(copies, 'row', 0, 0, axis_index_groups=chips, tiled=True)  12.4 us
    pallas_call x1, Pallas kernels, local(): pl.pallas_call(functools.partial(field_kernel, cells), out_shape=[pltpu.V...  10.9 us
    ppermute x8, waiting for transfers between devices, swap(): return lax.ppermute(value, 'row', [(i, i ^ distance) for i in range(size)])  9.51 us
    pallas_call x1, Pallas kernels, local(): pl.pallas_call(kv_kernel, out_shape=[pltpu.VMEM(kv_shape, F32)] * 2 + [pl...  9.36 us
    ppermute x8, starting transfers between devices, swap(): return lax.ppermute(value, 'row', [(i, i ^ distance) for i in range(size)])  8.28 us
    pallas_call x1, Pallas kernels, local(): pl.pallas_call(functools.partial(last_kernel, cells), out_shape=jax.Shape...  5.55 us
    pallas_call x1, Pallas kernels, local(): pl.pallas_call(query_kernel, out_shape=pltpu.VMEM(field.shape, BF16), gri...  2.38 us
  transfers between devices with their start and end apart: 8, of which 7 were waited for; matrix products, arithmetic and copies ran while one was open for 0% of the time, Pallas kernels for 3%

commit v1 on v0

--- a/solution.py
+++ b/solution.py
@@ -16,6 +16,7 @@
 SUB = 512
 KV_SUB = 256
 LAST_SUB = 1024
+LAST_ROWS = 4
 ROWS = 2
 F32 = jnp.float32
 BF16 = jnp.bfloat16
@@ -97,7 +98,7 @@
 
 
 def kv_kernel(me_ref, far_ref, w_far, wa_ref, wi_ref, wo_ref, keep_ref, send_ref, x_ref, w_ref, wa_near, wi_near, wo_near,
-              w_t, normed, acc, arrived, landed):
+              w_t, raw, normed, acc, arrived, landed):
     step = pl.program_id(0)
     channels = HEADS * HD
     fetches = [
@@ -116,15 +117,15 @@
             row_copy(row).start()
         for fetch in fetches:
             fetch.start()
+        raw[...] = jnp.zeros_like(raw)
         normed[...] = jnp.zeros_like(normed)
         acc[...] = jnp.zeros_like(acc)
         weights.wait()
         w_t[...] = w_ref[:, channels:].T
 
-    row_copy(step).wait()
-    acc[...] += mm_nt(normed[:channels, :], normed[channels:, :])
-
-    def project(block, _):
+    blocks = x_ref.shape[1] // KV_SUB
+
+    def project(block):
         return mm_nt(w_t[...], x_ref[step, block * KV_SUB : (block + 1) * KV_SUB, :])
 
     def normalize(block, both):
@@ -134,10 +135,21 @@
         scaled = center * lax.rsqrt(spread)
         normed[:, block * KV_SUB : (block + 1) * KV_SUB] = scaled.reshape(2 * channels, KV_SUB).astype(BF16)
 
-    skewed([project, normalize], x_ref.shape[1] // KV_SUB)
+    row_copy(step).wait()
+    here = project(0)
+    normalize(blocks - 1, raw[...])
+    acc[...] += mm_nt(normed[:channels, :], normed[channels:, :])
+    ahead = project(1)
+    for block in range(blocks - 1):
+        normalize(block, here)
+        here = ahead
+        if block + 2 < blocks:
+            ahead = project(block + 2)
+    raw[...] = here
 
     @pl.when(step == pl.num_programs(0) - 1)
     def _():
+        normalize(blocks - 1, raw[...])
         total = acc[...] + mm_nt(normed[:channels, :], normed[channels:, :])
         left = lax.broadcasted_iota(jnp.int32, (HD, 2 * HD), 1) < HD
         pairs = []
@@ -265,30 +277,34 @@
             found = mm(ang_ref[me_ref[1]], jnp.concatenate([both, both], axis=0))
             split(back, pl.ds(kw, 2 * rows, stride=MW), found * ((2.0 if kw else 1.0) / cells))
 
-    there = pl.ds(pl.multiple_of(step * 2 * MW, 2 * MW), 2 * MW)
-    rhs = jnp.concatenate([ws_ref[...], join(back, there, range(back.shape[0])).astype(BF16)], axis=0)
+    parts = second_ref.shape[1] // LAST_SUB
+
+    def send(row, part):
+        here = pl.ds(part * LAST_SUB, LAST_SUB)
+        return pltpu.make_async_copy(held.at[row, here], out_ref.at[row, here], sent.at[row, part])
+
+    def place(block):
+        return step * LAST_ROWS + block // parts, block % parts
 
     def both(block, _):
-        here = slice(block * LAST_SUB, (block + 1) * LAST_SUB)
-        return mm(jnp.concatenate([second_ref[step, here, :], tab_ref[here, :]], axis=1), rhs)
-
-    blocks = second_ref.shape[1] // LAST_SUB
-
-    def send(row, block):
-        here = pl.ds(block * LAST_SUB, LAST_SUB)
-        return pltpu.make_async_copy(held.at[row, here], out_ref.at[row, here], sent.at[row, block])
+        row, part = place(block)
+        here = slice(part * LAST_SUB, (part + 1) * LAST_SUB)
+        there = pl.ds(pl.multiple_of(row * 2 * MW, 2 * MW), 2 * MW)
+        rhs = jnp.concatenate([ws_ref[...], join(back, there, range(back.shape[0])).astype(BF16)], axis=0)
+        return mm(jnp.concatenate([second_ref[row, here, :], tab_ref[here, :]], axis=1), rhs)
 
     def finish(block, value):
-        held[step, block * LAST_SUB : (block + 1) * LAST_SUB, :] = gelu(value).astype(BF16)
-        send(step, block).start()
-
-    skewed([both, finish], blocks)
+        row, part = place(block)
+        held[row, part * LAST_SUB : (part + 1) * LAST_SUB, :] = gelu(value).astype(BF16)
+        send(row, part).start()
+
+    skewed([both, finish], LAST_ROWS * parts)
 
     @pl.when(step == pl.num_programs(0) - 1)
     def _():
         for row in range(rows):
-            for block in range(blocks):
-                send(row, block).wait()
+            for part in range(parts):
+                send(row, part).wait()
 
 
 def near(value):
@@ -334,6 +350,7 @@
             out_specs=[HERE] * 7,
             scratch_shapes=[
                 pltpu.VMEM((2 * channels, channels), BF16),
+                pltpu.VMEM((2 * channels, KV_SUB), F32),
                 pltpu.VMEM((2 * channels, columns), BF16),
                 pltpu.VMEM((channels, channels), F32),
                 pltpu.SemaphoreType.DMA((4,)),
@@ -412,7 +429,7 @@
         out_shape=jax.ShapeDtypeStruct(field.shape, BF16),
         grid_spec=pltpu.PrefetchScalarGridSpec(
             num_scalar_prefetch=1,
-            grid=(strip_rows,),
+            grid=(strip_rows // LAST_ROWS,),
             in_specs=[HERE] * 6,
             out_specs=hbm,
             scratch_shapes=[

time: 74.7 us -> 73.9 us (0.989)
  Pallas kernels: 29.7 us -> 28.9 us
where the time goes in v1:
time: 73.9 us; the launch traced here: 73.7 us
  Pallas kernels  28.9 us (39%)
  blocking collectives  26.8 us (36%)
  waiting for transfers between devices  9.5 us (13%)
  starting transfers between devices  8.28 us (11%)
    all_to_all x1, blocking collectives, local(): lax.all_to_all(both, 'row', 0, 0, axis_index_groups=chips, tiled=True)  14.4 us
    all_to_all x1, blocking collectives, local(): lax.all_to_all(copies, 'row', 0, 0, axis_index_groups=chips, tiled=True)  12.4 us
    pallas_call x1, Pallas kernels, local(): pl.pallas_call(functools.partial(field_kernel, cells), out_shape=[pltpu.V...  10.9 us
    ppermute x8, waiting for transfers between devices, swap(): return lax.ppermute(value, 'row', [(i, i ^ distance) for i in range(size)])  9.5 us
    pallas_call x1, Pallas kernels, local(): pl.pallas_call(kv_kernel, out_shape=[pltpu.VMEM(kv_shape, F32)] * 2 + [pl...  8.9 us
    ppermute x8, starting transfers between devices, swap(): return lax.ppermute(value, 'row', [(i, i ^ distance) for i in range(size)])  8.28 us
    pallas_call x1, Pallas kernels, local(): pl.pallas_call(functools.partial(last_kernel, cells), out_shape=jax.Shape...  5.18 us
    pallas_call x1, Pallas kernels, local(): pl.pallas_call(query_kernel, out_shape=pltpu.VMEM(field.shape, BF16), gri...  2.38 us
  transfers between devices with their start and end apart: 8, of which 7 were waited for; matrix products, arithmetic and copies ran while one was open for 0% of the time, Pallas kernels for 3%

profile of v1, /device:TPU:0, one launch (start us, length us, event | category | flops | bytes accessed | tf_op | source)
XLA Modules:
  0.0 73.7 jit_solution(14965099070343436918)
XLA Ops:
  0.0 0.1 pad_add_fusion.me_ref
  0.1 8.9 %kv.1 = (f32[64,128]{1,0:T(8,128)S(1)}, f32[64,128]{1,0:T(8,128)S(1)}, bf16[8,1024,256]{2,1,0:T(8,128)(2,1)S(1)}, bf16[256,768]{1,0:T(8,128)(2,1)S(1)}, bf16[256...) custom-call(s32[2]{0:T(128)S(1)} %pad_add_fusion.me_ref, ...), custom_call_target="tpu_custom_call" | custom-call | tf_op jit(solution)/shard_map/kv/pallas_call | solution.py:343
  9.0 0.6 collective-permute-start
  9.5 0.9 %collective-permute-done = f32[64,128]{1,0:T(8,128)S(1)} collective-permute-done((f32[64,128]{1,0:T(8,128)S(1)}, f32[64,128]{1,0:T(8,128)S(1)}, u32[]{:S(2)}, u32[]{:S(2)}) %collective-permute-start) | collective-permute-done | bytes 32800 | tf_op jit(solution)/shard_map/ppermute | solution.py:334
  10.4 3.9 %collective-permute-start.3 = (f32[64,128]{1,0:T(8,128)S(1)}, f32[64,128]{1,0:T(8,128)S(1)}, u32[]{:S(2)}, u32[]{:S(2)}) collective-permute-start(f32[64,128]{1,0:T(8,128)S(1)} %add.18), channel_id=1, source_target_pairs={{0,6},{1,7},{2,4},{3,5},{4,2},{5,3},{6,0},{7,1},{8,14},{9,15},{10,... | collective-permute-start | bytes 98312 | tf_op jit(solution)/shard_map/ppermute | solution.py:334
  14.3 0.4 collective-permute-start.2
  14.7 0.2 collective-permute-start.1
  14.9 1.3 %collective-permute-done.3 = f32[64,128]{1,0:T(8,128)S(1)} collective-permute-done((f32[64,128]{1,0:T(8,128)S(1)}, f32[64,128]{1,0:T(8,128)S(1)}, u32[]{:S(2)}, u32[]{:S(2)}) %collective-permute-start.3) | collective-permute-done | bytes 32800 | tf_op jit(solution)/shard_map/ppermute | solution.py:334
  16.2 2.0 %collective-permute-done.2 = f32[64,128]{1,0:T(8,128)S(1)} collective-permute-done((f32[64,128]{1,0:T(8,128)S(1)}, f32[64,128]{1,0:T(8,128)S(1)}, u32[]{:S(2)}, u32[]{:S(2)}) %collective-permute-start.2) | collective-permute-done | bytes 32800 | tf_op jit(solution)/shard_map/ppermute | solution.py:334
  18.2 0.4 collective-permute-done.1
  18.6 2.7 %collective-permute-start.4 = (f32[64,128]{1,0:T(8,128)S(1)}, f32[64,128]{1,0:T(8,128)S(1)}, u32[]{:S(2)}, u32[]{:S(2)}) collective-permute-start(f32[64,128]{1,0:T(8,128)S(1)} %add_add_fusion), channel_id=1, source_target_pairs={{0,8},{1,9},{2,10},{3,11},{4,12},{5,13},{6,14},{7,15},{8,0},{9,1},... | collective-permute-start | bytes 98312 | tf_op jit(solution)/shard_map/ppermute | solution.py:334
  21.3 2.2 %collective-permute-done.4 = f32[64,128]{1,0:T(8,128)S(1)} collective-permute-done((f32[64,128]{1,0:T(8,128)S(1)}, f32[64,128]{1,0:T(8,128)S(1)}, u32[]{:S(2)}, u32[]{:S(2)}) %collective-permute-start.4) | collective-permute-done | bytes 32800 | tf_op jit(solution)/shard_map/ppermute | solution.py:334
  23.5 0.0 collective-permute-start.5
  23.5 0.0 copy-start
  23.6 0.0 copy-start.4
  23.6 2.4 %qproj.1.ask_ref = bf16[8,1024,256]{2,1,0:T(8,128)(2,1)S(1)} custom-call(bf16[8,1024,256]{2,1,0:T(8,128)(2,1)S(1)} %get-tuple-element.16.x_ref, bf16[256,768]{1,0:T(8,128)(2,1)S(1)} %get-tuple-element.19.w_ref), custom_call_target="tpu_custom_call" | custom-call | flops 1073741824 | bytes 8388608 | tf_op jit(solution)/shard_map/qproj/pallas_call | solution.py:363
  26.0 0.0 collective-permute-done.5.kvb_ref
  26.0 0.0 copy-done
  26.0 0.0 copy-done.4
  26.0 10.9 %field.1 = (bf16[8,1024,256]{2,1,0:T(8,128)(2,1)S(1)}, f32[8,32,512]{2,1,0:T(8,128)S(1)}, bf16[8,32,512]{2,1,0:T(8,128)(2,1)S(1)}, bf16[32,512,256]{2,1,0:T(8,128)(2,1)S(1)}) custom-call(s32[2]{0:T(128)S(1)} %pad_add_fusion.me_ref, bf16[8,1024,256]{2,1,0:T(8,128)(2,1)S(1)} %get-tuple-element.16.x_ref, f32[64,128]{1,0:T(8,128)S(1)} %add.22.kva_ref, ...), custom_call_target="tpu_custom_call" | custom-call | tf_op jit(solution)/shard_map/field/pallas_call | solution.py:386
  36.9 0.6 collective-permute-start.6
  37.4 1.2 %collective-permute-done.6 = bf16[8,32,512]{2,1,0:T(8,128)(2,1)S(1)} collective-permute-done((bf16[8,32,512]{2,1,0:T(8,128)(2,1)S(1)}, bf16[8,32,512]{2,1,0:T(8,128)(2,1)S(1)}, u32[]{:S(2)}, u32[]{:S(2)}) %collective-permute-start.6) | collective-permute-done | bytes 262176 | tf_op jit(solution)/shard_map/ppermute | solution.py:334
  38.6 0.1 add_convert_fusion
  38.7 14.4 %all_to_all.10.terms_ref = bf16[8,32,512]{2,1,0:T(8,128)(2,1)S(1)} all-to-all(bf16[8,32,512]{2,1,0:T(8,128)(2,1)S(1)} %add_convert_fusion), channel_id=1, replica_groups={{0,2,4,6,8,10,12,14},{1,3,5,7,9,11,13,15},{16,18,20,22,24,26,28,30},{17..., dimensions={0} | all-to-all | bytes 524288 | tf_op jit(solution)/shard_map/all_to_all | solution.py:411
  53.0 1.6 %modes.1 = bf16[8,32,512]{2,1,0:T(8,128)(2,1)S(1)} custom-call(bf16[8,32,512]{2,1,0:T(8,128)(2,1)S(1)} %all_to_all.10.terms_ref, bf16[32,512,256]{2,1,0:T(8,128)(2,1)S(1)} %get-tuple-element.26.w_ref), custom_call_target="tpu_custom_call" | custom-call | tf_op jit(solution)/shard_map/modes/pallas_call | solution.py:414
  54.6 12.4 %all_to_all.11.lo_ref = bf16[8,32,512]{2,1,0:T(8,128)(2,1)S(1)} all-to-all(bf16[8,32,512]{2,1,0:T(8,128)(2,1)S(1)} %modes.1), channel_id=1, replica_groups={{0,2,4,6,8,10,12,14},{1,3,5,7,9,11,13,15},{16,18,20,22,24,26,28,30},{17..., dimensions={0} | all-to-all | bytes 524288 | tf_op jit(solution)/shard_map/all_to_all | solution.py:424
  67.0 0.0 collective-permute-start.7
  67.0 1.5 %collective-permute-done.7.hi_ref = bf16[8,32,512]{2,1,0:T(8,128)(2,1)S(1)} collective-permute-done((bf16[8,32,512]{2,1,0:T(8,128)(2,1)S(1)}, bf16[8,32,512]{2,1,0:T(8,128)(2,1)S(1)}, u32[]{:S(2)}, u32[]{:S(2)}) %collective-permute-start.7) | collective-permute-done | bytes 262176 | tf_op jit(solution)/shard_map/ppermute | solution.py:334
  68.6 0.0 copy-done.1
  68.6 0.0 copy-done.2
  68.6 0.0 copy-done.3
  68.6 5.2 %last.1 = bf16[8,1024,256]{2,1,0:T(8,128)(2,1)} custom-call(s32[2]{0:T(128)S(1)} %pad_add_fusion.me_ref, bf16[8,1024,256]{2,1,0:T(8,128)(2,1)S(1)} %get-tuple-element.23.second_ref, bf16[8,32,512]{2,1,0:T(8,128)(2,1)S(1)} %all_to_all.11.lo_ref, bf16[8,32,512]{2,1,0:T(8,128)(2,1)S(1)} %collective-permute-done.7.hi_ref, bf16[256,256]{1,0:T(8,128)(2,1)S(1)} %copy-done.2, ...), custom_call_target="tpu_custom_call" | custom-call | tf_op jit(solution)/shard_map/last/pallas_call | solution.py:427
  (6 shorter events, 0.0 us)
Async XLA Ops:
  9.0 1.4 %collective-permute-start = (f32[64,128]{1,0:T(8,128)S(1)}, f32[64,128]{1,0:T(8,128)S(1)}, u32[]{:S(2)}, u32[]{:S(2)}) collective-permute-start(f32[64,128]{1,0:T(8,128)S(1)} %get-tuple-element.18), channel_id=1, source_target_pairs={{0,1},{1,0},{2,3},{3,2},{4,5},{5,4},{6,7},{7,6},{8,9},{9,8},{10,11... | collective-permute-start | bytes 98312 | tf_op jit(solution)/shard_map/ppermute | solution.py:334
  10.4 5.8 %collective-permute-start.3 = (f32[64,128]{1,0:T(8,128)S(1)}, f32[64,128]{1,0:T(8,128)S(1)}, u32[]{:S(2)}, u32[]{:S(2)}) collective-permute-start(f32[64,128]{1,0:T(8,128)S(1)} %add.18), channel_id=1, source_target_pairs={{0,6},{1,7},{2,4},{3,5},{4,2},{5,3},{6,0},{7,1},{8,14},{9,15},{10,... | collective-permute-start | bytes 98312 | tf_op jit(solution)/shard_map/ppermute | solution.py:334
  14.3 3.9 %collective-permute-start.2 = (f32[64,128]{1,0:T(8,128)S(1)}, f32[64,128]{1,0:T(8,128)S(1)}, u32[]{:S(2)}, u32[]{:S(2)}) collective-permute-start(f32[64,128]{1,0:T(8,128)S(1)} %add.18), channel_id=1, source_target_pairs={{0,4},{1,5},{2,6},{3,7},{4,0},{5,1},{6,2},{7,3},{8,12},{9,13},{10,... | collective-permute-start | bytes 98312 | tf_op jit(solution)/shard_map/ppermute | solution.py:334
  14.7 3.9 %collective-permute-start.1 = (f32[64,128]{1,0:T(8,128)S(1)}, f32[64,128]{1,0:T(8,128)S(1)}, u32[]{:S(2)}, u32[]{:S(2)}) collective-permute-start(f32[64,128]{1,0:T(8,128)S(1)} %add.18), channel_id=1, source_target_pairs={{0,2},{1,3},{2,0},{3,1},{4,6},{5,7},{6,4},{7,5},{8,10},{9,11},{10,... | collective-permute-start | bytes 98312 | tf_op jit(solution)/shard_map/ppermute | solution.py:334
  18.6 4.9 %collective-permute-start.4 = (f32[64,128]{1,0:T(8,128)S(1)}, f32[64,128]{1,0:T(8,128)S(1)}, u32[]{:S(2)}, u32[]{:S(2)}) collective-permute-start(f32[64,128]{1,0:T(8,128)S(1)} %add_add_fusion), channel_id=1, source_target_pairs={{0,8},{1,9},{2,10},{3,11},{4,12},{5,13},{6,14},{7,15},{8,0},{9,1},... | collective-permute-start | bytes 98312 | tf_op jit(solution)/shard_map/ppermute | solution.py:334
  23.5 2.4 %collective-permute-start.5 = (f32[64,128]{1,0:T(8,128)S(1)}, f32[64,128]{1,0:T(8,128)S(1)}, u32[]{:S(2)}, u32[]{:S(2)}) collective-permute-start(f32[64,128]{1,0:T(8,128)S(1)} %add.22.kva_ref), channel_id=1, source_target_pairs={{0,1},{1,0},{2,3},{3,2},{4,5},{5,4},{6,7},{7,6},{8,9},{9,8},{10,11... | collective-permute-start | bytes 98312 | tf_op jit(solution)/shard_map/ppermute | solution.py:334
  23.5 2.4 %copy-start = (bf16[16,64,48]{2,1,0:T(8,128)(2,1)S(1)}, bf16[16,64,48]{2,1,0:T(8,128)(2,1)}, u32[]{:S(2)}) copy-start(bf16[16,64,48]{2,1,0:T(8,128)(2,1)} %constant.16.clone.ang_ref) | copy-start | bytes 294916
  23.6 2.4 %copy-start.4 = (bf16[32,1024]{1,0:T(8,128)(2,1)S(1)}, bf16[32,1024]{1,0:T(8,128)(2,1)}, u32[]{:S(2)}) copy-start(bf16[32,1024]{1,0:T(8,128)(2,1)} %constant.14.clone.tab_ref) | copy-start | bytes 196612
  36.9 1.7 %collective-permute-start.6 = (bf16[8,32,512]{2,1,0:T(8,128)(2,1)S(1)}, bf16[8,32,512]{2,1,0:T(8,128)(2,1)S(1)}, u32[]{:S(2)}, u32[]{:S(2)}) collective-permute-start(bf16[8,32,512]{2,1,0:T(8,128)(2,1)S(1)} %get-tuple-element.25), channel_id=1, source_target_pairs={{0,1},{1,0},{2,3},{3,2},{4,5},{5,4},{6,7},{7,6},{8,9},{9,8},{10,11... | collective-permute-start | bytes 786440 | tf_op jit(solution)/shard_map/ppermute | solution.py:334
  53.0 15.5 %copy-start.1 = (bf16[1024,32]{1,0:T(8,128)(2,1)S(1)}, bf16[1024,32]{1,0:T(8,128)(2,1)}, u32[]{:S(2)}) copy-start(bf16[1024,32]{1,0:T(8,128)(2,1)} %constant.15.clone.tab_ref) | copy-start | bytes 196612
  53.0 15.5 %copy-start.2 = (bf16[256,256]{1,0:T(8,128)(2,1)S(1)}, bf16[256,256]{1,0:T(8,128)(2,1)}, u32[]{:S(2)}) copy-start(bf16[256,256]{1,0:T(8,128)(2,1)} %ws_ref.1) | copy-start | bytes 393220
  53.0 15.5 %copy-start.3 = (bf16[16,16,128]{2,1,0:T(8,128)(2,1)S(1)}, bf16[16,16,128]{2,1,0:T(8,128)(2,1)}, u32[]{:S(2)}) copy-start(bf16[16,16,128]{2,1,0:T(8,128)(2,1)} %constant.17.clone.ang_ref) | copy-start | bytes 196612
  67.0 1.5 %collective-permute-start.7 = (bf16[8,32,512]{2,1,0:T(8,128)(2,1)S(1)}, bf16[8,32,512]{2,1,0:T(8,128)(2,1)S(1)}, u32[]{:S(2)}, u32[]{:S(2)}) collective-permute-start(bf16[8,32,512]{2,1,0:T(8,128)(2,1)S(1)} %all_to_all.11.lo_ref), channel_id=1, source_target_pairs={{0,1},{1,0},{2,3},{3,2},{4,5},{5,4},{6,7},{7,6},{8,9},{9,8},{10,11... | collective-permute-start | bytes 786440 | tf_op jit(solution)/shard_map/ppermute | solution.py:334

commit v2 on v1

--- a/solution.py
+++ b/solution.py
@@ -15,9 +15,9 @@
 EPSILON = 1e-05
 SUB = 512
 KV_SUB = 256
-LAST_SUB = 1024
-LAST_ROWS = 4
-ROWS = 2
+LAST_SUB = 512
+LAST_ROWS = 8
+ROWS = 4
 F32 = jnp.float32
 BF16 = jnp.bfloat16
 

time: 73.9 us -> 73.1 us (0.989)
  Pallas kernels: 28.9 us -> 28 us
where the time goes in v2:
time: 73.1 us; the launch traced here: 72.9 us
  Pallas kernels  28 us (38%)
  blocking collectives  26.8 us (37%)
  waiting for transfers between devices  9.5 us (13%)
  starting transfers between devices  8.28 us (11%)
    all_to_all x1, blocking collectives, local(): lax.all_to_all(both, 'row', 0, 0, axis_index_groups=chips, tiled=True)  14.4 us
    all_to_all x1, blocking collectives, local(): lax.all_to_all(copies, 'row', 0, 0, axis_index_groups=chips, tiled=True)  12.4 us
    pallas_call x1, Pallas kernels, local(): pl.pallas_call(functools.partial(field_kernel, cells), out_shape=[pltpu.V...  10.7 us
    ppermute x8, waiting for transfers between devices, swap(): return lax.ppermute(value, 'row', [(i, i ^ distance) for i in range(size)])  9.5 us
    pallas_call x1, Pallas kernels, local(): pl.pallas_call(kv_kernel, out_shape=[pltpu.VMEM(kv_shape, F32)] * 2 + [pl...  8.9 us
    ppermute x8, starting transfers between devices, swap(): return lax.ppermute(value, 'row', [(i, i ^ distance) for i in range(size)])  8.28 us
    pallas_call x1, Pallas kernels, local(): pl.pallas_call(functools.partial(last_kernel, cells), out_shape=jax.Shape...  4.47 us
    pallas_call x1, Pallas kernels, local(): pl.pallas_call(query_kernel, out_shape=pltpu.VMEM(field.shape, BF16), gri...  2.38 us
  transfers between devices with their start and end apart: 8, of which 7 were waited for; matrix products, arithmetic and copies ran while one was open for 0% of the time, Pallas kernels for 3%

profile of v2, /device:TPU:0, one launch (start us, length us, event | category | flops | bytes accessed | tf_op | source)
XLA Modules:
  0.0 72.9 jit_solution(6439758501061299361)
XLA Ops:
  0.0 0.1 pad_add_fusion.me_ref
  0.1 8.9 %kv.1 = (f32[64,128]{1,0:T(8,128)S(1)}, f32[64,128]{1,0:T(8,128)S(1)}, bf16[8,1024,256]{2,1,0:T(8,128)(2,1)S(1)}, bf16[256,768]{1,0:T(8,128)(2,1)S(1)}, bf16[256...) custom-call(s32[2]{0:T(128)S(1)} %pad_add_fusion.me_ref, ...), custom_call_target="tpu_custom_call" | custom-call | tf_op jit(solution)/shard_map/kv/pallas_call | solution.py:343
  9.0 0.6 collective-permute-start
  9.5 0.9 %collective-permute-done = f32[64,128]{1,0:T(8,128)S(1)} collective-permute-done((f32[64,128]{1,0:T(8,128)S(1)}, f32[64,128]{1,0:T(8,128)S(1)}, u32[]{:S(2)}, u32[]{:S(2)}) %collective-permute-start) | collective-permute-done | bytes 32800 | tf_op jit(solution)/shard_map/ppermute | solution.py:334
  10.4 3.9 %collective-permute-start.3 = (f32[64,128]{1,0:T(8,128)S(1)}, f32[64,128]{1,0:T(8,128)S(1)}, u32[]{:S(2)}, u32[]{:S(2)}) collective-permute-start(f32[64,128]{1,0:T(8,128)S(1)} %add.18), channel_id=1, source_target_pairs={{0,6},{1,7},{2,4},{3,5},{4,2},{5,3},{6,0},{7,1},{8,14},{9,15},{10,... | collective-permute-start | bytes 98312 | tf_op jit(solution)/shard_map/ppermute | solution.py:334
  14.3 0.4 collective-permute-start.2
  14.7 0.2 collective-permute-start.1
  14.9 1.3 %collective-permute-done.3 = f32[64,128]{1,0:T(8,128)S(1)} collective-permute-done((f32[64,128]{1,0:T(8,128)S(1)}, f32[64,128]{1,0:T(8,128)S(1)}, u32[]{:S(2)}, u32[]{:S(2)}) %collective-permute-start.3) | collective-permute-done | bytes 32800 | tf_op jit(solution)/shard_map/ppermute | solution.py:334
  16.2 2.0 %collective-permute-done.2 = f32[64,128]{1,0:T(8,128)S(1)} collective-permute-done((f32[64,128]{1,0:T(8,128)S(1)}, f32[64,128]{1,0:T(8,128)S(1)}, u32[]{:S(2)}, u32[]{:S(2)}) %collective-permute-start.2) | collective-permute-done | bytes 32800 | tf_op jit(solution)/shard_map/ppermute | solution.py:334
  18.2 0.4 collective-permute-done.1
  18.6 2.7 %collective-permute-start.4 = (f32[64,128]{1,0:T(8,128)S(1)}, f32[64,128]{1,0:T(8,128)S(1)}, u32[]{:S(2)}, u32[]{:S(2)}) collective-permute-start(f32[64,128]{1,0:T(8,128)S(1)} %add_add_fusion), channel_id=1, source_target_pairs={{0,8},{1,9},{2,10},{3,11},{4,12},{5,13},{6,14},{7,15},{8,0},{9,1},... | collective-permute-start | bytes 98312 | tf_op jit(solution)/shard_map/ppermute | solution.py:334
  21.3 2.2 %collective-permute-done.4 = f32[64,128]{1,0:T(8,128)S(1)} collective-permute-done((f32[64,128]{1,0:T(8,128)S(1)}, f32[64,128]{1,0:T(8,128)S(1)}, u32[]{:S(2)}, u32[]{:S(2)}) %collective-permute-start.4) | collective-permute-done | bytes 32800 | tf_op jit(solution)/shard_map/ppermute | solution.py:334
  23.5 0.0 collective-permute-start.5
  23.5 0.0 copy-start
  23.6 0.0 copy-start.4
  23.6 2.4 %qproj.1.ask_ref = bf16[8,1024,256]{2,1,0:T(8,128)(2,1)S(1)} custom-call(bf16[8,1024,256]{2,1,0:T(8,128)(2,1)S(1)} %get-tuple-element.16.x_ref, bf16[256,768]{1,0:T(8,128)(2,1)S(1)} %get-tuple-element.19.w_ref), custom_call_target="tpu_custom_call" | custom-call | flops 1073741824 | bytes 8388608 | tf_op jit(solution)/shard_map/qproj/pallas_call | solution.py:363
  26.0 0.0 collective-permute-done.5.kvb_ref
  26.0 0.0 copy-done
  26.0 0.0 copy-done.4
  26.0 10.7 %field.1 = (bf16[8,1024,256]{2,1,0:T(8,128)(2,1)S(1)}, f32[8,32,512]{2,1,0:T(8,128)S(1)}, bf16[8,32,512]{2,1,0:T(8,128)(2,1)S(1)}, bf16[32,512,256]{2,1,0:T(8,128)(2,1)S(1)}) custom-call(s32[2]{0:T(128)S(1)} %pad_add_fusion.me_ref, bf16[8,1024,256]{2,1,0:T(8,128)(2,1)S(1)} %get-tuple-element.16.x_ref, f32[64,128]{1,0:T(8,128)S(1)} %add.22.kva_ref, ...), custom_call_target="tpu_custom_call" | custom-call | tf_op jit(solution)/shard_map/field/pallas_call | solution.py:386
  36.7 0.6 collective-permute-start.6
  37.3 1.2 %collective-permute-done.6 = bf16[8,32,512]{2,1,0:T(8,128)(2,1)S(1)} collective-permute-done((bf16[8,32,512]{2,1,0:T(8,128)(2,1)S(1)}, bf16[8,32,512]{2,1,0:T(8,128)(2,1)S(1)}, u32[]{:S(2)}, u32[]{:S(2)}) %collective-permute-start.6) | collective-permute-done | bytes 262176 | tf_op jit(solution)/shard_map/ppermute | solution.py:334
  38.4 0.1 add_convert_fusion
  38.5 14.4 %all_to_all.10.terms_ref = bf16[8,32,512]{2,1,0:T(8,128)(2,1)S(1)} all-to-all(bf16[8,32,512]{2,1,0:T(8,128)(2,1)S(1)} %add_convert_fusion), channel_id=1, replica_groups={{0,2,4,6,8,10,12,14},{1,3,5,7,9,11,13,15},{16,18,20,22,24,26,28,30},{17..., dimensions={0} | all-to-all | bytes 524288 | tf_op jit(solution)/shard_map/all_to_all | solution.py:411
  52.9 1.6 %modes.1 = bf16[8,32,512]{2,1,0:T(8,128)(2,1)S(1)} custom-call(bf16[8,32,512]{2,1,0:T(8,128)(2,1)S(1)} %all_to_all.10.terms_ref, bf16[32,512,256]{2,1,0:T(8,128)(2,1)S(1)} %get-tuple-element.26.w_ref), custom_call_target="tpu_custom_call" | custom-call | tf_op jit(solution)/shard_map/modes/pallas_call | solution.py:414
  54.4 12.4 %all_to_all.11.lo_ref = bf16[8,32,512]{2,1,0:T(8,128)(2,1)S(1)} all-to-all(bf16[8,32,512]{2,1,0:T(8,128)(2,1)S(1)} %modes.1), channel_id=1, replica_groups={{0,2,4,6,8,10,12,14},{1,3,5,7,9,11,13,15},{16,18,20,22,24,26,28,30},{17..., dimensions={0} | all-to-all | bytes 524288 | tf_op jit(solution)/shard_map/all_to_all | solution.py:424
  66.9 0.0 collective-permute-start.7
  66.9 1.5 %collective-permute-done.7.hi_ref = bf16[8,32,512]{2,1,0:T(8,128)(2,1)S(1)} collective-permute-done((bf16[8,32,512]{2,1,0:T(8,128)(2,1)S(1)}, bf16[8,32,512]{2,1,0:T(8,128)(2,1)S(1)}, u32[]{:S(2)}, u32[]{:S(2)}) %collective-permute-start.7) | collective-permute-done | bytes 262176 | tf_op jit(solution)/shard_map/ppermute | solution.py:334
  68.4 0.0 copy-done.1
  68.4 0.0 copy-done.2
  68.4 0.0 copy-done.3
  68.4 4.5 %last.1 = bf16[8,1024,256]{2,1,0:T(8,128)(2,1)} custom-call(s32[2]{0:T(128)S(1)} %pad_add_fusion.me_ref, bf16[8,1024,256]{2,1,0:T(8,128)(2,1)S(1)} %get-tuple-element.23.second_ref, bf16[8,32,512]{2,1,0:T(8,128)(2,1)S(1)} %all_to_all.11.lo_ref, bf16[8,32,512]{2,1,0:T(8,128)(2,1)S(1)} %collective-permute-done.7.hi_ref, bf16[256,256]{1,0:T(8,128)(2,1)S(1)} %copy-done.2, ...), custom_call_target="tpu_custom_call" | custom-call | tf_op jit(solution)/shard_map/last/pallas_call | solution.py:427
  (6 shorter events, 0.0 us)
Async XLA Ops:
  9.0 1.4 %collective-permute-start = (f32[64,128]{1,0:T(8,128)S(1)}, f32[64,128]{1,0:T(8,128)S(1)}, u32[]{:S(2)}, u32[]{:S(2)}) collective-permute-start(f32[64,128]{1,0:T(8,128)S(1)} %get-tuple-element.18), channel_id=1, source_target_pairs={{0,1},{1,0},{2,3},{3,2},{4,5},{5,4},{6,7},{7,6},{8,9},{9,8},{10,11... | collective-permute-start | bytes 98312 | tf_op jit(solution)/shard_map/ppermute | solution.py:334
  10.4 5.8 %collective-permute-start.3 = (f32[64,128]{1,0:T(8,128)S(1)}, f32[64,128]{1,0:T(8,128)S(1)}, u32[]{:S(2)}, u32[]{:S(2)}) collective-permute-start(f32[64,128]{1,0:T(8,128)S(1)} %add.18), channel_id=1, source_target_pairs={{0,6},{1,7},{2,4},{3,5},{4,2},{5,3},{6,0},{7,1},{8,14},{9,15},{10,... | collective-permute-start | bytes 98312 | tf_op jit(solution)/shard_map/ppermute | solution.py:334
  14.3 3.9 %collective-permute-start.2 = (f32[64,128]{1,0:T(8,128)S(1)}, f32[64,128]{1,0:T(8,128)S(1)}, u32[]{:S(2)}, u32[]{:S(2)}) collective-permute-start(f32[64,128]{1,0:T(8,128)S(1)} %add.18), channel_id=1, source_target_pairs={{0,4},{1,5},{2,6},{3,7},{4,0},{5,1},{6,2},{7,3},{8,12},{9,13},{10,... | collective-permute-start | bytes 98312 | tf_op jit(solution)/shard_map/ppermute | solution.py:334
  14.7 3.9 %collective-permute-start.1 = (f32[64,128]{1,0:T(8,128)S(1)}, f32[64,128]{1,0:T(8,128)S(1)}, u32[]{:S(2)}, u32[]{:S(2)}) collective-permute-start(f32[64,128]{1,0:T(8,128)S(1)} %add.18), channel_id=1, source_target_pairs={{0,2},{1,3},{2,0},{3,1},{4,6},{5,7},{6,4},{7,5},{8,10},{9,11},{10,... | collective-permute-start | bytes 98312 | tf_op jit(solution)/shard_map/ppermute | solution.py:334
  18.6 4.9 %collective-permute-start.4 = (f32[64,128]{1,0:T(8,128)S(1)}, f32[64,128]{1,0:T(8,128)S(1)}, u32[]{:S(2)}, u32[]{:S(2)}) collective-permute-start(f32[64,128]{1,0:T(8,128)S(1)} %add_add_fusion), channel_id=1, source_target_pairs={{0,8},{1,9},{2,10},{3,11},{4,12},{5,13},{6,14},{7,15},{8,0},{9,1},... | collective-permute-start | bytes 98312 | tf_op jit(solution)/shard_map/ppermute | solution.py:334
  23.5 2.4 %collective-permute-start.5 = (f32[64,128]{1,0:T(8,128)S(1)}, f32[64,128]{1,0:T(8,128)S(1)}, u32[]{:S(2)}, u32[]{:S(2)}) collective-permute-start(f32[64,128]{1,0:T(8,128)S(1)} %add.22.kva_ref), channel_id=1, source_target_pairs={{0,1},{1,0},{2,3},{3,2},{4,5},{5,4},{6,7},{7,6},{8,9},{9,8},{10,11... | collective-permute-start | bytes 98312 | tf_op jit(solution)/shard_map/ppermute | solution.py:334
  23.5 2.4 %copy-start = (bf16[16,64,48]{2,1,0:T(8,128)(2,1)S(1)}, bf16[16,64,48]{2,1,0:T(8,128)(2,1)}, u32[]{:S(2)}) copy-start(bf16[16,64,48]{2,1,0:T(8,128)(2,1)} %constant.16.clone.ang_ref) | copy-start | bytes 294916
  23.6 2.4 %copy-start.4 = (bf16[32,1024]{1,0:T(8,128)(2,1)S(1)}, bf16[32,1024]{1,0:T(8,128)(2,1)}, u32[]{:S(2)}) copy-start(bf16[32,1024]{1,0:T(8,128)(2,1)} %constant.14.clone.tab_ref) | copy-start | bytes 196612
  36.7 1.7 %collective-permute-start.6 = (bf16[8,32,512]{2,1,0:T(8,128)(2,1)S(1)}, bf16[8,32,512]{2,1,0:T(8,128)(2,1)S(1)}, u32[]{:S(2)}, u32[]{:S(2)}) collective-permute-start(bf16[8,32,512]{2,1,0:T(8,128)(2,1)S(1)} %get-tuple-element.25), channel_id=1, source_target_pairs={{0,1},{1,0},{2,3},{3,2},{4,5},{5,4},{6,7},{7,6},{8,9},{9,8},{10,11... | collective-permute-start | bytes 786440 | tf_op jit(solution)/shard_map/ppermute | solution.py:334
  52.9 15.5 %copy-start.1 = (bf16[1024,32]{1,0:T(8,128)(2,1)S(1)}, bf16[1024,32]{1,0:T(8,128)(2,1)}, u32[]{:S(2)}) copy-start(bf16[1024,32]{1,0:T(8,128)(2,1)} %constant.15.clone.tab_ref) | copy-start | bytes 196612
  52.9 15.5 %copy-start.2 = (bf16[256,256]{1,0:T(8,128)(2,1)S(1)}, bf16[256,256]{1,0:T(8,128)(2,1)}, u32[]{:S(2)}) copy-start(bf16[256,256]{1,0:T(8,128)(2,1)} %ws_ref.1) | copy-start | bytes 393220
  52.9 15.5 %copy-start.3 = (bf16[16,16,128]{2,1,0:T(8,128)(2,1)S(1)}, bf16[16,16,128]{2,1,0:T(8,128)(2,1)}, u32[]{:S(2)}) copy-start(bf16[16,16,128]{2,1,0:T(8,128)(2,1)} %constant.17.clone.ang_ref) | copy-start | bytes 196612
  66.9 1.5 %collective-permute-start.7 = (bf16[8,32,512]{2,1,0:T(8,128)(2,1)S(1)}, bf16[8,32,512]{2,1,0:T(8,128)(2,1)S(1)}, u32[]{:S(2)}, u32[]{:S(2)}) collective-permute-start(bf16[8,32,512]{2,1,0:T(8,128)(2,1)S(1)} %all_to_all.11.lo_ref), channel_id=1, source_target_pairs={{0,1},{1,0},{2,3},{3,2},{4,5},{5,4},{6,7},{7,6},{8,9},{9,8},{10,11... | collective-permute-start | bytes 786440 | tf_op jit(solution)/shard_map/ppermute | solution.py:334
